TPU v7x, 32 devices: a whole 2x2x4 slice. The times are simulated.
32 devices in a mesh: shot: 4 (over y, core), recv: 8 (over z, x).
Axes of the slice: x: 2, y: 2, z: 4, core: 2. Of those that a mesh axis runs over, the one named last changes fastest.
Arguments:
- wavefield: bfloat16 [2, 8, 1, 1024, 4096], P(None, 'recv', None, None, 'shot'), may hold values from -1 to 1
- live: int32 [4096], replicated, may hold values 0 or 1
- block_order: int32 [32], replicated, may hold values from 0 to 31, each once
- wavelet: float32 [2, 2], replicated, may hold values from 0.5 to 1.5
Outputs:
- multiples: bfloat16 [2, 8, 1, 1024, 4096], P(None, 'recv', None, None, 'shot')
Inputs may be any that keep to these rules, and one draw needn't show every extreme that they name: `block_order`: each block number appears once.
All inputs are finite; a program needn't handle non-finite values.
Results may differ from a plain program's by a relative error of at most 0.001.
Values may be sent and summed in bfloat16 or wider, within the bound.
No kernel may reach another device: no remote copies, remote signals or barrier semaphores. Data moves between devices by JAX's collectives and lax.ppermute only.
A program may use at most 64 MiB of HBM per device.

v0:
```python
import jax
import jax.numpy as jnp
from jax import lax
from jax.sharding import PartitionSpec as P

BLOCK = 128
RGROUPS = 4
ROUNDS = 2
BPR = 2


def spread(block, axis, holder):
    block = jnp.where(lax.axis_index(axis) == holder, block, jnp.zeros_like(block))
    return lax.psum(block, axis)


def partner(block, axis, apart):
    count = lax.axis_size(axis)
    route = []
    for low in range(count):
        high = low | 1 << apart
        if high != low and high < count:
            route += [(low, high), (high, low)]
    return lax.ppermute(block, axis, route)


def accumulate(total, columns, rows):

    def product(first, second):
        return jnp.einsum("frk,fks->frs", first, second, preferred_element_type=jnp.float32)

    real = product(columns[0], rows[0]) - product(columns[1], rows[1])
    imag = product(columns[0], rows[1]) + product(columns[1], rows[0])
    return total + jnp.stack([real, imag])


def shards(wavefield, live, block_order, wavelet):
    tile = wavefield[:, 0]
    freq_dev = tile.shape[1]
    recv_rows = tile.shape[2]
    shot_cols = tile.shape[3]
    count = ROUNDS * BPR
    bits = RGROUPS.bit_length() - 1
    position = lax.axis_index("recv")
    my_group = position % RGROUPS
    freq_group = position // RGROUPS
    scales = lax.dynamic_slice_in_dim(wavelet, freq_group * freq_dev, freq_dev, 1)

    def own_rows(block):
        start = block * BLOCK
        owner = start // recv_rows
        offset = start % recv_rows
        piece = lax.dynamic_slice_in_dim(tile, offset, BLOCK, 2)
        return jnp.where(owner == my_group, piece, jnp.zeros_like(piece))

    def columns_of(block):
        start = block * BLOCK
        root = start // shot_cols
        offset = start % shot_cols
        mine = lax.dynamic_slice_in_dim(tile, offset, BLOCK, 3)
        columns = spread(mine, "shot", root)
        weight = lax.dynamic_slice_in_dim(live, start, BLOCK, 0).astype(jnp.bfloat16)
        return columns * weight[None, None, None, :]

    def rows_of(block):
        value = own_rows(block)
        for bit in range(bits):
            value = value + partner(value, "recv", bit)
        return value

    def fetch(step):
        block = block_order[step]
        return (columns_of(block), rows_of(block))

    empty = jnp.zeros((2, freq_dev, recv_rows, shot_cols), jnp.float32)

    def turn(step, carry):
        total, columns, rows = carry
        next_columns, next_rows = fetch(step + 1)
        return (accumulate(total, columns, rows), next_columns, next_rows)

    first_columns, first_rows = fetch(0)
    total, columns, rows = lax.fori_loop(0, count - 1, turn, (empty, first_columns, first_rows))
    total = accumulate(total, columns, rows)
    scale_re = scales[0][:, None, None]
    scale_im = scales[1][:, None, None]
    out_re = -(scale_re * total[0] - scale_im * total[1])
    out_im = -(scale_re * total[1] + scale_im * total[0])
    result = jnp.stack([out_re, out_im]).astype(jnp.bfloat16)
    return result[:, None]


def solution(mesh):
    placed = (P(None, "recv", None, None, "shot"), P(), P(), P())
    return jax.shard_map(
        shards,
        mesh=mesh,
        in_specs=placed,
        out_specs=P(None, "recv", None, None, "shot"),
        check_vma=False,
    )
```

profile of v0, /device:TPU:0, one launch (start us, length us, event | category | flops | bytes accessed | tf_op | source)
XLA Modules:
  0.0 183.8 jit_solution(3456191400455826749)
XLA Ops:
  7.3 1.2 select_bitcast_fusion
  8.5 3.0 %collective-permute-start.2 = (bf16[2,1,128,1024]{3,2,1,0:T(8,128)(2,1)S(1)}, bf16[2,1,128,1024]{3,2,1,0:T(8,128)(2,1)S(1)}, u32[]{:S(2)}, u32[]{:S(2)}) collective-permute-start(bf16[2,1,128,1024]{3,2,1,0:T(8,128)(2,1)S(1)} %select_bitcast_fusion), channel_id=1, source_target_pairs={{0,1},{1,0},{2,3},{3,2},{4,5},{5,4},{6,7},{7,6},{8,9},{9,8},{10,11... | collective-permute-start | bytes 1572872 | tf_op jit(solution)/shard_map/ppermute | solution.py:24
  11.6 2.3 %select_bitcast_fusion.1 = bf16[2,1,1024,128]{3,2,1,0:T(8,128)(2,1)} fusion(bf16[2,1,1,1024,1024]{4,3,0,2,1:T(8,128)(2,1)} %bitcast.89, s32[]{:T(128)S(6)} %select_n.175, pred[]{:T(512)S(6)} %eq.38), kind=kLoop, calls=%fused_computation.34 | loop fusion | flops 262144 | bytes 1048581 | tf_op jit(solution)/shard_map/jit(_where)/select_n | solution.py:13
  13.9 9.6 %collective-permute-done.2 = bf16[2,1,128,1024]{3,2,1,0:T(8,128)(2,1)S(1)} collective-permute-done((bf16[2,1,128,1024]{3,2,1,0:T(8,128)(2,1)S(1)}, bf16[2,1,128,1024]{3,2,1,0:T(8,128)(2,1)S(1)}, u32[]{:S(2)}, u32[]{:S(2)}) %collective-permute-start.2) | collective-permute-done | bytes 524320 | tf_op jit(solution)/shard_map/ppermute | solution.py:24
  23.5 1.3 fusion.40
  24.8 1.9 %collective-permute-start.3 = (bf16[2,1,128,1024]{3,2,1,0:T(8,128)(2,1)S(1)}, bf16[2,1,128,1024]{3,2,1,0:T(8,128)(2,1)S(1)}, u32[]{:S(2)}, u32[]{:S(2)}) collective-permute-start(bf16[2,1,128,1024]{3,2,1,0:T(8,128)(2,1)S(1)} %fusion.40), channel_id=1, source_target_pairs={{0,2},{2,0},{1,3},{3,1},{4,6},{6,4},{5,7},{7,5},{8,10},{10,8},{9,1... | collective-permute-start | bytes 1572872 | tf_op jit(solution)/shard_map/ppermute | solution.py:24
  28.2 19.6 %all-reduce.3.cloned.1.call-done = bf16[2,1,1024,128]{3,2,1,0:T(8,128)(2,1)} async-done(((bf16[2,1,1024,128]{3,2,1,0:T(8,128)(2,1)}), bf16[2,1,1024,128]{3,2,1,0:T(8,128)(2,1)}) %all-reduce.3.cloned.1.call-update) | async-done | bytes 524304 | tf_op jit(solution)/shard_map/psum | solution.py:14
  47.8 1.1 broadcast_multiply_fusion.1
  49.1 115.6 %while.20 = (s32[]{:T(128)}, f32[2,1,1024,1024]{3,2,1,0:T(8,128)}, bf16[2,1,1024,128]{3,2,1,0:T(8,128)(2,1)S(1)}, bf16[2,1,128,1024]{3,2,1,0:T(8,128)(2,1)S(1)},...) while((s32[]{:T(128)}, f32[2,1,1024,1024]{3,2,1,0:T(8,128)}, ...), condition=%wide.region_3.4_spmd.clone, body=%wide.region_1.3_spmd.clone.sunk | while | flops 1084752000 | bytes 82839248 | solution.py:83
  50.4 2.3 %dynamic-slice_select_fusion.4 = bf16[2,1,1024,128]{3,2,1,0:T(8,128)(2,1)} fusion(bf16[2,1,1024,1024]{3,2,1,0:T(8,128)(2,1)} %get-tuple-element.349, s32[]{:T(128)S(6)} %select_n.227, pred[]{:T(512)S(6)} %eq.44), kind=kLoop, calls=%fused_computation.4.clone.1 | loop fusion | flops 262144 | bytes 1048581 | tf_op jit(solution)/shard_map/while/body/eval_jaxpr/jit(_where)/select_n | solution.py:13
  52.7 1.2 dynamic-slice_select_fusion.5
  54.0 1.5 collective-permute-start
  55.5 2.7 %fusion.60 = f32[1024,1024]{1,0:T(8,128)} fusion(bf16[2,1,128,1024]{3,2,1,0:T(8,128)(2,1)S(1)} %get-tuple-element.329, bf16[2,1,1024,128]{3,2,1,0:T(8,128)(2,1)S(1)} %get-tuple-element.328), kind=kOutput, calls=%fused_computation.5.clone.1 | convolution fusion | flops 268435456 | bytes 4718592 | tf_op jit(solution)/shard_map/while/body/eval_jaxpr/frk,fks->frs/dot_general | solution.py:30
  58.2 2.7 %fusion.61 = f32[1024,1024]{1,0:T(8,128)} fusion(bf16[2,1,128,1024]{3,2,1,0:T(8,128)(2,1)S(1)} %get-tuple-element.329, bf16[2,1,1024,128]{3,2,1,0:T(8,128)(2,1)S(1)} %get-tuple-element.328), kind=kOutput, calls=%fused_computation.11.clone.1 | convolution fusion | flops 268435456 | bytes 4718592 | tf_op jit(solution)/shard_map/while/body/eval_jaxpr/frk,fks->frs/dot_general | solution.py:30
  60.9 3.1 %add_bitcast_fusion.3 = f32[1,1,1024,1024]{3,2,1,0:T(8,128)S(1)} fusion(f32[1024,1024]{1,0:T(8,128)} %fusion.60, bf16[2,1,1024,128]{3,2,1,0:T(8,128)(2,1)S(1)} %get-tuple-element.328, bf16[2,1,128,1024]{3,2,1,0:T(8,128)(2,1)S(1)} %get-tuple-element.329), kind=kOutput, calls=%fused_computation.1.clone.1 | convolution fusion | flops 269484032 | bytes 8912896 | tf_op jit(solution)/shard_map/while/body/eval_jaxpr/frk,fks->frs/dot_general | solution.py:30
  65.1 1.4 collective-permute-done
  66.5 1.3 fusion.62
  67.8 1.8 collective-permute-start.1
  69.6 4.2 %maximum_add_fusion.3 = f32[2,1,1024,1024]{3,2,1,0:T(8,128)} fusion(f32[1,1,1024,1024]{3,2,1,0:T(8,128)S(1)} %add_bitcast_fusion.3, f32[1,1,1024,1024]{3,2,1,0:T(8,128)S(1)} %subtract_bitcast_fusion.3, f32[2,1,1024,1024]{3,2,1,0:T(8,128)} %get-tuple-element.327, pred[]{:T(512)S(6)} %compare.20), kind=kLoop, calls=%fused_computation.clone.1 | loop fusion | flops 6291456 | bytes 25165824 | tf_op jit(solution)/shard_map/while/body/eval_jaxpr/add | solution.py:34
  74.6 11.8 %all-reduce.5.cloned.1.call-done = bf16[2,1,1024,128]{3,2,1,0:T(8,128)(2,1)} async-done(((bf16[2,1,1024,128]{3,2,1,0:T(8,128)(2,1)}), bf16[2,1,1024,128]{3,2,1,0:T(8,128)(2,1)}) %all-reduce.5.cloned.1.call-update) | async-done | bytes 524304 | tf_op jit(solution)/shard_map/while/body/eval_jaxpr/psum | solution.py:14
  86.4 1.1 broadcast_multiply_fusion.3
  89.0 2.3 %dynamic-slice_select_fusion.4 = bf16[2,1,1024,128]{3,2,1,0:T(8,128)(2,1)} fusion(bf16[2,1,1024,1024]{3,2,1,0:T(8,128)(2,1)} %get-tuple-element.349, s32[]{:T(128)S(6)} %select_n.227, pred[]{:T(512)S(6)} %eq.44), kind=kLoop, calls=%fused_computation.4.clone.1 | loop fusion | flops 262144 | bytes 1048581 | tf_op jit(solution)/shard_map/while/body/eval_jaxpr/jit(_where)/select_n | solution.py:13
  91.3 1.2 dynamic-slice_select_fusion.5
  92.6 1.5 collective-permute-start
  94.1 2.7 %fusion.60 = f32[1024,1024]{1,0:T(8,128)} fusion(bf16[2,1,128,1024]{3,2,1,0:T(8,128)(2,1)S(1)} %get-tuple-element.329, bf16[2,1,1024,128]{3,2,1,0:T(8,128)(2,1)S(1)} %get-tuple-element.328), kind=kOutput, calls=%fused_computation.5.clone.1 | convolution fusion | flops 268435456 | bytes 4718592 | tf_op jit(solution)/shard_map/while/body/eval_jaxpr/frk,fks->frs/dot_general | solution.py:30
  96.8 2.7 %fusion.61 = f32[1024,1024]{1,0:T(8,128)} fusion(bf16[2,1,128,1024]{3,2,1,0:T(8,128)(2,1)S(1)} %get-tuple-element.329, bf16[2,1,1024,128]{3,2,1,0:T(8,128)(2,1)S(1)} %get-tuple-element.328), kind=kOutput, calls=%fused_computation.11.clone.1 | convolution fusion | flops 268435456 | bytes 4718592 | tf_op jit(solution)/shard_map/while/body/eval_jaxpr/frk,fks->frs/dot_general | solution.py:30
  99.4 3.1 %add_bitcast_fusion.3 = f32[1,1,1024,1024]{3,2,1,0:T(8,128)S(1)} fusion(f32[1024,1024]{1,0:T(8,128)} %fusion.60, bf16[2,1,1024,128]{3,2,1,0:T(8,128)(2,1)S(1)} %get-tuple-element.328, bf16[2,1,128,1024]{3,2,1,0:T(8,128)(2,1)S(1)} %get-tuple-element.329), kind=kOutput, calls=%fused_computation.1.clone.1 | convolution fusion | flops 269484032 | bytes 8912896 | tf_op jit(solution)/shard_map/while/body/eval_jaxpr/frk,fks->frs/dot_general | solution.py:30
  103.7 1.5 collective-permute-done
  105.1 1.3 fusion.62
  106.5 1.8 collective-permute-start.1
  108.3 6.5 %maximum_add_fusion.3 = f32[2,1,1024,1024]{3,2,1,0:T(8,128)} fusion(f32[1,1,1024,1024]{3,2,1,0:T(8,128)S(1)} %add_bitcast_fusion.3, f32[1,1,1024,1024]{3,2,1,0:T(8,128)S(1)} %subtract_bitcast_fusion.3, f32[2,1,1024,1024]{3,2,1,0:T(8,128)} %get-tuple-element.327, pred[]{:T(512)S(6)} %compare.20), kind=kLoop, calls=%fused_computation.clone.1 | loop fusion | flops 6291456 | bytes 25165824 | tf_op jit(solution)/shard_map/while/body/eval_jaxpr/add | solution.py:34
  115.5 9.3 %all-reduce.5.cloned.1.call-done = bf16[2,1,1024,128]{3,2,1,0:T(8,128)(2,1)} async-done(((bf16[2,1,1024,128]{3,2,1,0:T(8,128)(2,1)}), bf16[2,1,1024,128]{3,2,1,0:T(8,128)(2,1)}) %all-reduce.5.cloned.1.call-update) | async-done | bytes 524304 | tf_op jit(solution)/shard_map/while/body/eval_jaxpr/psum | solution.py:14
  124.9 1.1 broadcast_multiply_fusion.3
  127.5 2.3 %dynamic-slice_select_fusion.4 = bf16[2,1,1024,128]{3,2,1,0:T(8,128)(2,1)} fusion(bf16[2,1,1024,1024]{3,2,1,0:T(8,128)(2,1)} %get-tuple-element.349, s32[]{:T(128)S(6)} %select_n.227, pred[]{:T(512)S(6)} %eq.44), kind=kLoop, calls=%fused_computation.4.clone.1 | loop fusion | flops 262144 | bytes 1048581 | tf_op jit(solution)/shard_map/while/body/eval_jaxpr/jit(_where)/select_n | solution.py:13
  129.8 1.2 dynamic-slice_select_fusion.5
  131.1 1.5 collective-permute-start
  132.6 2.7 %fusion.60 = f32[1024,1024]{1,0:T(8,128)} fusion(bf16[2,1,128,1024]{3,2,1,0:T(8,128)(2,1)S(1)} %get-tuple-element.329, bf16[2,1,1024,128]{3,2,1,0:T(8,128)(2,1)S(1)} %get-tuple-element.328), kind=kOutput, calls=%fused_computation.5.clone.1 | convolution fusion | flops 268435456 | bytes 4718592 | tf_op jit(solution)/shard_map/while/body/eval_jaxpr/frk,fks->frs/dot_general | solution.py:30
  135.3 2.7 %fusion.61 = f32[1024,1024]{1,0:T(8,128)} fusion(bf16[2,1,128,1024]{3,2,1,0:T(8,128)(2,1)S(1)} %get-tuple-element.329, bf16[2,1,1024,128]{3,2,1,0:T(8,128)(2,1)S(1)} %get-tuple-element.328), kind=kOutput, calls=%fused_computation.11.clone.1 | convolution fusion | flops 268435456 | bytes 4718592 | tf_op jit(solution)/shard_map/while/body/eval_jaxpr/frk,fks->frs/dot_general | solution.py:30
  138.0 3.1 %add_bitcast_fusion.3 = f32[1,1,1024,1024]{3,2,1,0:T(8,128)S(1)} fusion(f32[1024,1024]{1,0:T(8,128)} %fusion.60, bf16[2,1,1024,128]{3,2,1,0:T(8,128)(2,1)S(1)} %get-tuple-element.328, bf16[2,1,128,1024]{3,2,1,0:T(8,128)(2,1)S(1)} %get-tuple-element.329), kind=kOutput, calls=%fused_computation.1.clone.1 | convolution fusion | flops 269484032 | bytes 8912896 | tf_op jit(solution)/shard_map/while/body/eval_jaxpr/frk,fks->frs/dot_general | solution.py:30
  142.2 1.5 collective-permute-done
  143.7 1.3 fusion.62
  145.0 1.8 collective-permute-start.1
  146.8 6.5 %maximum_add_fusion.3 = f32[2,1,1024,1024]{3,2,1,0:T(8,128)} fusion(f32[1,1,1024,1024]{3,2,1,0:T(8,128)S(1)} %add_bitcast_fusion.3, f32[1,1,1024,1024]{3,2,1,0:T(8,128)S(1)} %subtract_bitcast_fusion.3, f32[2,1,1024,1024]{3,2,1,0:T(8,128)} %get-tuple-element.327, pred[]{:T(512)S(6)} %compare.20), kind=kLoop, calls=%fused_computation.clone.1 | loop fusion | flops 6291456 | bytes 25165824 | tf_op jit(solution)/shard_map/while/body/eval_jaxpr/add | solution.py:34
  154.0 9.3 %all-reduce.5.cloned.1.call-done = bf16[2,1,1024,128]{3,2,1,0:T(8,128)(2,1)} async-done(((bf16[2,1,1024,128]{3,2,1,0:T(8,128)(2,1)}), bf16[2,1,1024,128]{3,2,1,0:T(8,128)(2,1)}) %all-reduce.5.cloned.1.call-update) | async-done | bytes 524304 | tf_op jit(solution)/shard_map/while/body/eval_jaxpr/psum | solution.py:14
  163.4 1.1 broadcast_multiply_fusion.3
  167.5 4.7 %maximum_add_fusion.1 = f32[2,1,1024,1024]{3,2,1,0:T(8,128)S(1)} fusion(f32[2,1,1024,1024]{3,2,1,0:T(8,128)} %get-tuple-element.209, f32[1,1,1024,1024]{3,2,1,0:T(8,128)S(1)} %add_bitcast_fusion.1, f32[1,1,1024,1024]{3,2,1,0:T(8,128)S(1)} %subtract_bitcast_fusion.1), kind=kLoop, calls=%fused_computation.25 | loop fusion | flops 4194304 | bytes 25165824 | tf_op jit(solution)/shard_map/add | solution.py:34
  172.2 2.6 %fusion.18 = (bf16[1,1,1,1024,1024]{4,3,2,1,0:T(8,128)(2,1)S(1)}, bf16[1,1,1,1024,1024]{4,3,2,1,0:T(8,128)(2,1)S(1)}) fusion(f32[2,1,1024,1024]{3,2,1,0:T(8,128)S(1)} %maximum_add_fusion.1, f32[]{:T(128)} %bitcast.13, f32[]{:T(128)} %bitcast), kind=kLoop, calls=%fused_computation.31 | loop fusion | flops 10485760 | bytes 12582920 | tf_op jit(solution)/shard_map/stack | solution.py:89
  174.9 2.4 %pad_maximum_fusion = bf16[2,1,1,1024,1024]{4,3,2,1,0:T(8,128)(2,1)} fusion(bf16[1,1,1,1024,1024]{4,3,2,1,0:T(8,128)(2,1)S(1)} %get-tuple-element.256, bf16[1,1,1,1024,1024]{4,3,2,1,0:T(8,128)(2,1)S(1)} %get-tuple-element.255), kind=kLoop, calls=%fused_computation.26 | loop fusion | flops 2097152 | bytes 8388608 | tf_op jit(solution)/shard_map/stack | solution.py:89
  (45 shorter events, 12.7 us)
Async XLA Ops:
  6.5 21.0 %copy-start = (f32[2,2]{1,0:T(2,128)S(1)}, f32[2,2]{1,0:T(2,128)}, u32[]{:S(2)}) copy-start(f32[2,2]{1,0:T(2,128)} %param.9) | copy-start | bytes 52
  6.5 42.5 %copy-start.3 = (s32[32]{0:T(128)S(1)}, s32[32]{0:T(128)}, u32[]{:S(2)}) copy-start(s32[32]{0:T(128)} %param.8) | copy-start | bytes 388
  6.5 41.2 %all-reduce.3.cloned.1.call-start = ((), (), s32[]{:S(2)}) async-start(), calls=%async_computation | async-start | bytes 1048576 | tf_op jit(solution)/shard_map/psum | solution.py:14
  8.5 15.0 %collective-permute-start.2 = (bf16[2,1,128,1024]{3,2,1,0:T(8,128)(2,1)S(1)}, bf16[2,1,128,1024]{3,2,1,0:T(8,128)(2,1)S(1)}, u32[]{:S(2)}, u32[]{:S(2)}) collective-permute-start(bf16[2,1,128,1024]{3,2,1,0:T(8,128)(2,1)S(1)} %select_bitcast_fusion), channel_id=1, source_target_pairs={{0,1},{1,0},{2,3},{3,2},{4,5},{5,4},{6,7},{7,6},{8,9},{9,8},{10,11... | collective-permute-start | bytes 1572872 | tf_op jit(solution)/shard_map/ppermute | solution.py:24
  24.8 24.0 %collective-permute-start.3 = (bf16[2,1,128,1024]{3,2,1,0:T(8,128)(2,1)S(1)}, bf16[2,1,128,1024]{3,2,1,0:T(8,128)(2,1)S(1)}, u32[]{:S(2)}, u32[]{:S(2)}) collective-permute-start(bf16[2,1,128,1024]{3,2,1,0:T(8,128)(2,1)S(1)} %fusion.40), channel_id=1, source_target_pairs={{0,2},{2,0},{1,3},{3,1},{4,6},{6,4},{5,7},{7,5},{8,10},{10,8},{9,1... | collective-permute-start | bytes 1572872 | tf_op jit(solution)/shard_map/ppermute | solution.py:24
  49.1 37.3 %all-reduce.5.cloned.1.call-start = ((), (), s32[]{:S(2)}) async-start(), calls=%async_computation.1 | async-start | bytes 1048576 | tf_op jit(solution)/shard_map/while/body/eval_jaxpr/psum | solution.py:14
  54.0 12.5 %collective-permute-start = (bf16[2,1,128,1024]{3,2,1,0:T(8,128)(2,1)S(1)}, bf16[2,1,128,1024]{3,2,1,0:T(8,128)(2,1)S(1)}, u32[]{:S(2)}, u32[]{:S(2)}) collective-permute-start(bf16[2,1,128,1024]{3,2,1,0:T(8,128)(2,1)S(1)} %dynamic-slice_select_fusion.5), channel_id=1, source_target_pairs={{0,1},{1,0},{2,3},{3,2},{4,5},{5,4},{6,7},{7,6},{8,9},{9,8},{10,11... | collective-permute-start | bytes 1572872 | tf_op jit(solution)/shard_map/while/body/eval_jaxpr/ppermute | solution.py:24
  60.9 3.5 %copy-start.2 = (f32[1024,1024]{1,0:T(8,128)S(1)}, f32[1024,1024]{1,0:T(8,128)}, u32[]{:S(2)}) copy-start(f32[1024,1024]{1,0:T(8,128)} %fusion.61) | copy-start | bytes 12582916 | tf_op jit(solution)/shard_map/while
  67.8 19.6 %collective-permute-start.1 = (bf16[2,1,128,1024]{3,2,1,0:T(8,128)(2,1)S(1)}, bf16[2,1,128,1024]{3,2,1,0:T(8,128)(2,1)S(1)}, u32[]{:S(2)}, u32[]{:S(2)}) collective-permute-start(bf16[2,1,128,1024]{3,2,1,0:T(8,128)(2,1)S(1)} %fusion.62), channel_id=1, source_target_pairs={{0,2},{2,0},{1,3},{3,1},{4,6},{6,4},{5,7},{7,5},{8,10},{10,8},{9,1... | collective-permute-start | bytes 1572872 | tf_op jit(solution)/shard_map/while/body/eval_jaxpr/ppermute | solution.py:24
  87.7 37.2 %all-reduce.5.cloned.1.call-start = ((), (), s32[]{:S(2)}) async-start(), calls=%async_computation.1 | async-start | bytes 1048576 | tf_op jit(solution)/shard_map/while/body/eval_jaxpr/psum | solution.py:14
  92.6 12.6 %collective-permute-start = (bf16[2,1,128,1024]{3,2,1,0:T(8,128)(2,1)S(1)}, bf16[2,1,128,1024]{3,2,1,0:T(8,128)(2,1)S(1)}, u32[]{:S(2)}, u32[]{:S(2)}) collective-permute-start(bf16[2,1,128,1024]{3,2,1,0:T(8,128)(2,1)S(1)} %dynamic-slice_select_fusion.5), channel_id=1, source_target_pairs={{0,1},{1,0},{2,3},{3,2},{4,5},{5,4},{6,7},{7,6},{8,9},{9,8},{10,11... | collective-permute-start | bytes 1572872 | tf_op jit(solution)/shard_map/while/body/eval_jaxpr/ppermute | solution.py:24
  99.4 3.5 %copy-start.2 = (f32[1024,1024]{1,0:T(8,128)S(1)}, f32[1024,1024]{1,0:T(8,128)}, u32[]{:S(2)}) copy-start(f32[1024,1024]{1,0:T(8,128)} %fusion.61) | copy-start | bytes 12582916 | tf_op jit(solution)/shard_map/while
  106.5 19.5 %collective-permute-start.1 = (bf16[2,1,128,1024]{3,2,1,0:T(8,128)(2,1)S(1)}, bf16[2,1,128,1024]{3,2,1,0:T(8,128)(2,1)S(1)}, u32[]{:S(2)}, u32[]{:S(2)}) collective-permute-start(bf16[2,1,128,1024]{3,2,1,0:T(8,128)(2,1)S(1)} %fusion.62), channel_id=1, source_target_pairs={{0,2},{2,0},{1,3},{3,1},{4,6},{6,4},{5,7},{7,5},{8,10},{10,8},{9,1... | collective-permute-start | bytes 1572872 | tf_op jit(solution)/shard_map/while/body/eval_jaxpr/ppermute | solution.py:24
  126.2 37.2 %all-reduce.5.cloned.1.call-start = ((), (), s32[]{:S(2)}) async-start(), calls=%async_computation.1 | async-start | bytes 1048576 | tf_op jit(solution)/shard_map/while/body/eval_jaxpr/psum | solution.py:14
  131.1 12.6 %collective-permute-start = (bf16[2,1,128,1024]{3,2,1,0:T(8,128)(2,1)S(1)}, bf16[2,1,128,1024]{3,2,1,0:T(8,128)(2,1)S(1)}, u32[]{:S(2)}, u32[]{:S(2)}) collective-permute-start(bf16[2,1,128,1024]{3,2,1,0:T(8,128)(2,1)S(1)} %dynamic-slice_select_fusion.5), channel_id=1, source_target_pairs={{0,1},{1,0},{2,3},{3,2},{4,5},{5,4},{6,7},{7,6},{8,9},{9,8},{10,11... | collective-permute-start | bytes 1572872 | tf_op jit(solution)/shard_map/while/body/eval_jaxpr/ppermute | solution.py:24
  138.0 3.5 %copy-start.2 = (f32[1024,1024]{1,0:T(8,128)S(1)}, f32[1024,1024]{1,0:T(8,128)}, u32[]{:S(2)}) copy-start(f32[1024,1024]{1,0:T(8,128)} %fusion.61) | copy-start | bytes 12582916 | tf_op jit(solution)/shard_map/while
  145.0 19.5 %collective-permute-start.1 = (bf16[2,1,128,1024]{3,2,1,0:T(8,128)(2,1)S(1)}, bf16[2,1,128,1024]{3,2,1,0:T(8,128)(2,1)S(1)}, u32[]{:S(2)}, u32[]{:S(2)}) collective-permute-start(bf16[2,1,128,1024]{3,2,1,0:T(8,128)(2,1)S(1)} %fusion.62), channel_id=1, source_target_pairs={{0,2},{2,0},{1,3},{3,1},{4,6},{6,4},{5,7},{7,5},{8,10},{10,8},{9,1... | collective-permute-start | bytes 1572872 | tf_op jit(solution)/shard_map/while/body/eval_jaxpr/ppermute | solution.py:24
  174.9 2.4 %copy-start.1 = (f32[2,2]{1,0:T(2,128)S(1)}, f32[2,2]{1,0:T(2,128)}, u32[]{:S(2)}) copy-start(f32[2,2]{1,0:T(2,128)} %param.9) | copy-start | bytes 52
Sparse Core Ops, SparseCore 0:
  14.0 33.7 all-reduce.2
  52.9 33.4 all-reduce.4
  91.4 33.3 all-reduce.4
  130.0 33.3 all-reduce.4
where the time goes:
time: 185 us; the launch traced here: 184 us
  waiting for transfers between devices  64.2 us (35%)
  other arithmetic  54.4 us (29%)
  matrix products  30.1 us (16%)
  starting transfers between devices  15.1 us (8%)
  between operations  14 us (8%)
  local copies, waits for them, and re-layouts  3.74 us (2%)
  loops' own time  2.35 us (1%)
    psum x4, waiting for transfers between devices, spread(): return lax.psum(block, axis)  50.1 us
    dot_general x16, matrix products, product(): jnp.einsum('frk,fks->frs', first, second, preferred_element_type=jnp.floa...  30.1 us
    add x4, other arithmetic, accumulate(): return total + jnp.stack([real, imag])  21.9 us
    ppermute x8, starting transfers between devices, partner(): return lax.ppermute(block, axis, route)  15 us
    ppermute x8, waiting for transfers between devices, partner(): return lax.ppermute(block, axis, route)  14 us
    select_n x4, other arithmetic, spread(): jnp.where(lax.axis_index(axis) == holder, block, jnp.zeros_like(block))  9.12 us
    add x8, other arithmetic, rows_of(): value = value + partner(value, 'recv', bit)  6.04 us
    another operation x2, other arithmetic, shards(): result = jnp.stack([out_re, out_im]).astype(jnp.bfloat16)  5.02 us
  transfers between devices with their start and end apart: 12, of which 8 were waited for; matrix products, arithmetic and copies ran while one was open for 35% of the time, Pallas kernels for 0%

commit v1 on v0

--- a/solution.py
+++ b/solution.py
@@ -11,7 +11,7 @@
 
 def spread(block, axis, holder):
     block = jnp.where(lax.axis_index(axis) == holder, block, jnp.zeros_like(block))
-    return lax.psum(block, axis)
+    return jnp.sum(lax.all_gather(block, axis), axis=0)
 
 
 def partner(block, axis, apart):

time: 185 us -> 162 us (0.88)
  matrix products: 30.1 us -> 13.3 us
  local copies, waits for them, and re-layouts: 3.74 us -> 13.7 us
  waiting for transfers between devices: 64.2 us -> 55.9 us
  other arithmetic: 54.4 us -> 47.5 us
    psum x4 -> x0, waiting for transfers between devices: 50.1 us -> none  [spread(): return lax.psum(block, axis)]
    ppermute x8, waiting for transfers between devices: 14 us -> 55.8 us  [partner(): return lax.ppermute(block, axis, route)]
    dot_general x16, matrix products: 30.1 us -> 13.3 us  [product(): jnp.einsum('frk,fks->frs', first, second, preferred_element_type=jnp.floa...]
    add x4, other arithmetic: 21.9 us -> 11.5 us  [accumulate(): return total + jnp.stack([real, imag])]
    while x6 -> x18, local copies, waits for them, and re-layouts: 1.29 us -> 9.72 us
    reduce_sum x0 -> x4, other arithmetic: none -> 7.75 us  [spread(): return jnp.sum(lax.all_gather(block, axis), axis=0)]
    mul x4, other arithmetic: 4.31 us -> 0.16 us  [columns_of(): return columns * weight[None, None, None, :]]
  transfers between devices with their start and end apart: 12 -> 12, of which waited for: 8 -> 8; matrix products, arithmetic and copies ran while one was open for 35% -> 19% of each run, Pallas kernels for 0% -> 0%
where the time goes in v1:
time: 162 us; the launch traced here: 161 us
  waiting for transfers between devices  55.9 us (35%)
  other arithmetic  47.5 us (29%)
  between operations  13.9 us (9%)
  starting transfers between devices  13.8 us (9%)
  local copies, waits for them, and re-layouts  13.7 us (8%)
  matrix products  13.3 us (8%)
  loops' own time  2.47 us (2%)
    ppermute x8, waiting for transfers between devices, partner(): return lax.ppermute(block, axis, route)  55.8 us
    ppermute x8, starting transfers between devices, partner(): return lax.ppermute(block, axis, route)  13.7 us
    dot_general x16, matrix products, product(): jnp.einsum('frk,fks->frs', first, second, preferred_element_type=jnp.floa...  13.3 us
    add x4, other arithmetic, accumulate(): return total + jnp.stack([real, imag])  11.5 us
    while x18, local copies, waits for them, and re-layouts  9.72 us
    select_n x4, other arithmetic, spread(): jnp.where(lax.axis_index(axis) == holder, block, jnp.zeros_like(block))  9.07 us
    reduce_sum x4, other arithmetic, spread(): return jnp.sum(lax.all_gather(block, axis), axis=0)  7.75 us
    add x8, other arithmetic, rows_of(): value = value + partner(value, 'recv', bit)  6.04 us
  transfers between devices with their start and end apart: 12, of which 8 were waited for; matrix products, arithmetic and copies ran while one was open for 19% of the time, Pallas kernels for 0%

profile of v1, /device:TPU:0, one launch (start us, length us, event | category | flops | bytes accessed | tf_op | source)
XLA Modules:
  0.0 160.6 jit_solution(237408483377770300)
XLA Ops:
  7.2 2.3 %dynamic-slice_select_fusion.2 = bf16[2,1,1,1024,128]{4,3,2,1,0:T(8,128)(2,1)} fusion(bf16[2,1,1,1024,1024]{4,3,2,1,0:T(8,128)(2,1)} %param.6, s32[]{:T(128)S(6)} %select_n.176, pred[]{:T(512)S(6)} %eq.38), kind=kLoop, calls=%fused_computation.36 | loop fusion | flops 262144 | bytes 1048581 | tf_op jit(solution)/shard_map/jit(_where)/select_n | solution.py:13
  9.6 1.2 select_bitcast_fusion
  10.8 3.0 %collective-permute-start.2 = (bf16[2,1,128,1024]{3,2,1,0:T(8,128)(2,1)S(1)}, bf16[2,1,128,1024]{3,2,1,0:T(8,128)(2,1)S(1)}, u32[]{:S(2)}, u32[]{:S(2)}) collective-permute-start(bf16[2,1,128,1024]{3,2,1,0:T(8,128)(2,1)S(1)} %select_bitcast_fusion), channel_id=1, source_target_pairs={{0,1},{1,0},{2,3},{3,2},{4,5},{5,4},{6,7},{7,6},{8,9},{9,8},{10,11... | collective-permute-start | bytes 1572872 | tf_op jit(solution)/shard_map/ppermute | solution.py:24
  13.8 11.9 %collective-permute-done.2 = bf16[2,1,128,1024]{3,2,1,0:T(8,128)(2,1)S(1)} collective-permute-done((bf16[2,1,128,1024]{3,2,1,0:T(8,128)(2,1)S(1)}, bf16[2,1,128,1024]{3,2,1,0:T(8,128)(2,1)S(1)}, u32[]{:S(2)}, u32[]{:S(2)}) %collective-permute-start.2) | collective-permute-done | bytes 524320 | tf_op jit(solution)/shard_map/ppermute | solution.py:24
  25.7 1.3 fusion.40
  27.1 1.9 %collective-permute-start.3 = (bf16[2,1,128,1024]{3,2,1,0:T(8,128)(2,1)S(1)}, bf16[2,1,128,1024]{3,2,1,0:T(8,128)(2,1)S(1)}, u32[]{:S(2)}, u32[]{:S(2)}) collective-permute-start(bf16[2,1,128,1024]{3,2,1,0:T(8,128)(2,1)S(1)} %fusion.40), channel_id=1, source_target_pairs={{0,2},{2,0},{1,3},{3,1},{4,6},{6,4},{5,7},{7,5},{8,10},{10,8},{9,1... | collective-permute-start | bytes 1572872 | tf_op jit(solution)/shard_map/ppermute | solution.py:24
  29.0 0.8 dynamic-slice_convert_fusion.1
  30.3 10.0 %collective-permute-done.3 = bf16[2,1,128,1024]{3,2,1,0:T(8,128)(2,1)S(1)} collective-permute-done((bf16[2,1,128,1024]{3,2,1,0:T(8,128)(2,1)S(1)}, bf16[2,1,128,1024]{3,2,1,0:T(8,128)(2,1)S(1)}, u32[]{:S(2)}, u32[]{:S(2)}) %collective-permute-start.3) | collective-permute-done | bytes 524320 | tf_op jit(solution)/shard_map/ppermute | solution.py:24
  40.6 2.1 %reduce.10 = bf16[2,1024,128]{2,1,0:T(8,128)(2,1)S(1)} reduce(bf16[4,2,1024,128]{3,2,1,0:T(8,128)(2,1)} %bitcast.105, bf16[]{:T(256)} %constant.206.clone.1), dimensions={0}, to_apply=%region_0.1 | reduce | flops 786432 | bytes 2621442 | tf_op jit(solution)/shard_map/reduce_sum | solution.py:14
  42.7 95.9 %while.20 = (s32[]{:T(128)}, f32[2,1,1024,1024]{3,2,1,0:T(8,128)}, bf16[2,1,1024,128]{3,2,0,1:T(8,128)(2,1)S(1)}, bf16[2,1,128,1024]{3,2,1,0:T(8,128)(2,1)S(1)},...) while((s32[]{:T(128)}, f32[2,1,1024,1024]{3,2,1,0:T(8,128)}, ...), condition=%wide.region_3.4_spmd.clone, body=%wide.region_1.3_spmd.clone.sunk | while | flops 1085276288 | bytes 132122368 | solution.py:83
  44.1 2.3 %dynamic-slice_select_fusion.5 = bf16[2,1,1024,128]{3,2,1,0:T(8,128)(2,1)} fusion(bf16[2,1,1024,1024]{3,2,1,0:T(8,128)(2,1)} %get-tuple-element.350, s32[]{:T(128)S(6)} %select_n.228, pred[]{:T(512)S(6)} %eq.44), kind=kLoop, calls=%fused_computation.6.clone.1 | loop fusion | flops 262144 | bytes 1048581 | tf_op jit(solution)/shard_map/while/body/eval_jaxpr/jit(_where)/select_n | solution.py:13
  46.4 1.2 dynamic-slice_select_fusion.6
  47.6 1.5 collective-permute-start
  49.1 0.8 dynamic-slice_convert_fusion.3
  52.7 7.3 %collective-permute-done = bf16[2,1,128,1024]{3,2,1,0:T(8,128)(2,1)S(1)} collective-permute-done((bf16[2,1,128,1024]{3,2,1,0:T(8,128)(2,1)S(1)}, bf16[2,1,128,1024]{3,2,1,0:T(8,128)(2,1)S(1)}, u32[]{:S(2)}, u32[]{:S(2)}) %collective-permute-start) | collective-permute-done | bytes 524320 | tf_op jit(solution)/shard_map/while/body/eval_jaxpr/ppermute | solution.py:24
  60.0 1.3 fusion.62
  61.3 1.3 collective-permute-start.1
  62.6 2.5 %maximum_add_fusion.3 = f32[2,1,1024,1024]{3,2,1,0:T(8,128)S(1)} fusion(f32[1,1,1024,1024]{3,2,1,0:T(8,128)S(1)} %add_bitcast_fusion.3, f32[1,1,1024,1024]{3,2,1,0:T(8,128)S(1)} %subtract_bitcast_fusion.3, f32[2,1,1024,1024]{3,2,1,0:T(8,128)S(1)} %bitcast.98, pred[]{:T(512)S(6)} %compare.20), kind=kLoop, calls=%fused_computation.clone.1 | loop fusion | flops 6291456 | bytes 25165824 | tf_op jit(solution)/shard_map/while/body/eval_jaxpr/add | solution.py:34
  65.2 3.2 %copy-done.2 = f32[2,1,1024,1024]{3,2,1,0:T(8,128)} copy-done((f32[2,1,1024,1024]{3,2,1,0:T(8,128)}, f32[2,1,1024,1024]{3,2,1,0:T(8,128)S(1)}, u32[]{:S(2)}) %copy-start.2) | copy-done | bytes 8388632 | tf_op jit(solution)/shard_map/while
  68.4 4.4 %collective-permute-done.1 = bf16[2,1,128,1024]{3,2,1,0:T(8,128)(2,1)S(1)} collective-permute-done((bf16[2,1,128,1024]{3,2,1,0:T(8,128)(2,1)S(1)}, bf16[2,1,128,1024]{3,2,1,0:T(8,128)(2,1)S(1)}, u32[]{:S(2)}, u32[]{:S(2)}) %collective-permute-start.1) | collective-permute-done | bytes 524320 | tf_op jit(solution)/shard_map/while/body/eval_jaxpr/ppermute | solution.py:24
  73.1 1.9 %bitcast_reduce_fusion.2 = bf16[2,1024,128]{2,1,0:T(8,128)(2,1)S(1)} fusion(bf16[4,2,1024,128]{3,2,1,0:T(8,128)(2,1)} %bitcast.101), kind=kLoop, calls=%fused_computation.3.clone.1 | loop fusion | flops 786432 | bytes 2621440 | tf_op jit(solution)/shard_map/while/body/eval_jaxpr/reduce_sum | solution.py:14
  76.4 2.3 %dynamic-slice_select_fusion.5 = bf16[2,1,1024,128]{3,2,1,0:T(8,128)(2,1)} fusion(bf16[2,1,1024,1024]{3,2,1,0:T(8,128)(2,1)} %get-tuple-element.350, s32[]{:T(128)S(6)} %select_n.228, pred[]{:T(512)S(6)} %eq.44), kind=kLoop, calls=%fused_computation.6.clone.1 | loop fusion | flops 262144 | bytes 1048581 | tf_op jit(solution)/shard_map/while/body/eval_jaxpr/jit(_where)/select_n | solution.py:13
  78.7 1.2 dynamic-slice_select_fusion.6
  79.9 1.0 collective-permute-start
  80.9 0.8 dynamic-slice_convert_fusion.3
  84.5 6.7 %collective-permute-done = bf16[2,1,128,1024]{3,2,1,0:T(8,128)(2,1)S(1)} collective-permute-done((bf16[2,1,128,1024]{3,2,1,0:T(8,128)(2,1)S(1)}, bf16[2,1,128,1024]{3,2,1,0:T(8,128)(2,1)S(1)}, u32[]{:S(2)}, u32[]{:S(2)}) %collective-permute-start) | collective-permute-done | bytes 524320 | tf_op jit(solution)/shard_map/while/body/eval_jaxpr/ppermute | solution.py:24
  91.2 1.3 fusion.62
  92.5 1.6 collective-permute-start.1
  94.1 2.5 %maximum_add_fusion.3 = f32[2,1,1024,1024]{3,2,1,0:T(8,128)S(1)} fusion(f32[1,1,1024,1024]{3,2,1,0:T(8,128)S(1)} %add_bitcast_fusion.3, f32[1,1,1024,1024]{3,2,1,0:T(8,128)S(1)} %subtract_bitcast_fusion.3, f32[2,1,1024,1024]{3,2,1,0:T(8,128)S(1)} %bitcast.98, pred[]{:T(512)S(6)} %compare.20), kind=kLoop, calls=%fused_computation.clone.1 | loop fusion | flops 6291456 | bytes 25165824 | tf_op jit(solution)/shard_map/while/body/eval_jaxpr/add | solution.py:34
  96.7 3.2 %copy-done.2 = f32[2,1,1024,1024]{3,2,1,0:T(8,128)} copy-done((f32[2,1,1024,1024]{3,2,1,0:T(8,128)}, f32[2,1,1024,1024]{3,2,1,0:T(8,128)S(1)}, u32[]{:S(2)}) %copy-start.2) | copy-done | bytes 8388632 | tf_op jit(solution)/shard_map/while
  99.9 3.4 %collective-permute-done.1 = bf16[2,1,128,1024]{3,2,1,0:T(8,128)(2,1)S(1)} collective-permute-done((bf16[2,1,128,1024]{3,2,1,0:T(8,128)(2,1)S(1)}, bf16[2,1,128,1024]{3,2,1,0:T(8,128)(2,1)S(1)}, u32[]{:S(2)}, u32[]{:S(2)}) %collective-permute-start.1) | collective-permute-done | bytes 524320 | tf_op jit(solution)/shard_map/while/body/eval_jaxpr/ppermute | solution.py:24
  103.5 1.9 %bitcast_reduce_fusion.2 = bf16[2,1024,128]{2,1,0:T(8,128)(2,1)S(1)} fusion(bf16[4,2,1024,128]{3,2,1,0:T(8,128)(2,1)} %bitcast.101), kind=kLoop, calls=%fused_computation.3.clone.1 | loop fusion | flops 786432 | bytes 2621440 | tf_op jit(solution)/shard_map/while/body/eval_jaxpr/reduce_sum | solution.py:14
  106.8 2.3 %dynamic-slice_select_fusion.5 = bf16[2,1,1024,128]{3,2,1,0:T(8,128)(2,1)} fusion(bf16[2,1,1024,1024]{3,2,1,0:T(8,128)(2,1)} %get-tuple-element.350, s32[]{:T(128)S(6)} %select_n.228, pred[]{:T(512)S(6)} %eq.44), kind=kLoop, calls=%fused_computation.6.clone.1 | loop fusion | flops 262144 | bytes 1048581 | tf_op jit(solution)/shard_map/while/body/eval_jaxpr/jit(_where)/select_n | solution.py:13
  109.1 1.2 dynamic-slice_select_fusion.6
  110.3 1.8 %collective-permute-start = (bf16[2,1,128,1024]{3,2,1,0:T(8,128)(2,1)S(1)}, bf16[2,1,128,1024]{3,2,1,0:T(8,128)(2,1)S(1)}, u32[]{:S(2)}, u32[]{:S(2)}) collective-permute-start(bf16[2,1,128,1024]{3,2,1,0:T(8,128)(2,1)S(1)} %dynamic-slice_select_fusion.6), channel_id=1, source_target_pairs={{0,1},{1,0},{2,3},{3,2},{4,5},{5,4},{6,7},{7,6},{8,9},{9,8},{10,11... | collective-permute-start | bytes 1572872 | tf_op jit(solution)/shard_map/while/body/eval_jaxpr/ppermute | solution.py:24
  112.1 0.8 dynamic-slice_convert_fusion.3
  115.7 7.4 %collective-permute-done = bf16[2,1,128,1024]{3,2,1,0:T(8,128)(2,1)S(1)} collective-permute-done((bf16[2,1,128,1024]{3,2,1,0:T(8,128)(2,1)S(1)}, bf16[2,1,128,1024]{3,2,1,0:T(8,128)(2,1)S(1)}, u32[]{:S(2)}, u32[]{:S(2)}) %collective-permute-start) | collective-permute-done | bytes 524320 | tf_op jit(solution)/shard_map/while/body/eval_jaxpr/ppermute | solution.py:24
  123.1 1.3 fusion.62
  124.4 1.6 collective-permute-start.1
  126.0 2.5 %maximum_add_fusion.3 = f32[2,1,1024,1024]{3,2,1,0:T(8,128)S(1)} fusion(f32[1,1,1024,1024]{3,2,1,0:T(8,128)S(1)} %add_bitcast_fusion.3, f32[1,1,1024,1024]{3,2,1,0:T(8,128)S(1)} %subtract_bitcast_fusion.3, f32[2,1,1024,1024]{3,2,1,0:T(8,128)S(1)} %bitcast.98, pred[]{:T(512)S(6)} %compare.20), kind=kLoop, calls=%fused_computation.clone.1 | loop fusion | flops 6291456 | bytes 25165824 | tf_op jit(solution)/shard_map/while/body/eval_jaxpr/add | solution.py:34
  128.5 3.2 %copy-done.2 = f32[2,1,1024,1024]{3,2,1,0:T(8,128)} copy-done((f32[2,1,1024,1024]{3,2,1,0:T(8,128)}, f32[2,1,1024,1024]{3,2,1,0:T(8,128)S(1)}, u32[]{:S(2)}) %copy-start.2) | copy-done | bytes 8388632 | tf_op jit(solution)/shard_map/while
  131.8 4.7 %collective-permute-done.1 = bf16[2,1,128,1024]{3,2,1,0:T(8,128)(2,1)S(1)} collective-permute-done((bf16[2,1,128,1024]{3,2,1,0:T(8,128)(2,1)S(1)}, bf16[2,1,128,1024]{3,2,1,0:T(8,128)(2,1)S(1)}, u32[]{:S(2)}, u32[]{:S(2)}) %collective-permute-start.1) | collective-permute-done | bytes 524320 | tf_op jit(solution)/shard_map/while/body/eval_jaxpr/ppermute | solution.py:24
  136.7 1.9 %bitcast_reduce_fusion.2 = bf16[2,1024,128]{2,1,0:T(8,128)(2,1)S(1)} fusion(bf16[4,2,1024,128]{3,2,1,0:T(8,128)(2,1)} %bitcast.101), kind=kLoop, calls=%fused_computation.3.clone.1 | loop fusion | flops 786432 | bytes 2621440 | tf_op jit(solution)/shard_map/while/body/eval_jaxpr/reduce_sum | solution.py:14
  140.7 2.8 %subtract_bitcast_fusion.1 = f32[1,1,1024,1024]{3,2,1,0:T(8,128)} fusion(f32[1024,1024]{1,0:T(8,128)S(1)} %fusion.26, bf16[2,1,128,1024]{3,2,1,0:T(8,128)(2,1)S(1)} %get-tuple-element.212, bf16[2,1,1024,128]{3,2,0,1:T(8,128)(2,1)S(1)} %get-tuple-element.211), kind=kOutput, calls=%fused_computation.31 | convolution fusion | flops 269484032 | bytes 8912896 | tf_op jit(solution)/shard_map/frk,fks->frs/dot_general | solution.py:30
  143.6 1.6 %slice-done.3 = s8[4194304]{0:T(1024)(128)(4,1)S(1)} async-done(((s8[8388608]{0:T(1024)(128)(4,1)}), s8[4194304]{0:T(1024)(128)(4,1)S(1)}, s32[]{:S(2)}) %slice-start.3) | async-done | bytes 4194328
  145.2 3.9 %maximum_add_fusion.1 = f32[2,1,1024,1024]{3,2,1,0:T(8,128)S(1)} fusion(f32[2,1,1024,1024]{3,2,1,0:T(8,128)S(1)} %bitcast.100, f32[1,1,1024,1024]{3,2,1,0:T(8,128)S(1)} %add_bitcast_fusion.1, f32[1,1,1024,1024]{3,2,1,0:T(8,128)} %subtract_bitcast_fusion.1), kind=kLoop, calls=%fused_computation.26 | loop fusion | flops 4194304 | bytes 25165824 | tf_op jit(solution)/shard_map/add | solution.py:34
  149.1 2.6 %fusion.18 = (bf16[1,1,1,1024,1024]{4,3,2,1,0:T(8,128)(2,1)S(1)}, bf16[1,1,1,1024,1024]{4,3,2,1,0:T(8,128)(2,1)S(1)}) fusion(f32[2,1,1024,1024]{3,2,1,0:T(8,128)S(1)} %maximum_add_fusion.1, f32[]{:T(128)} %bitcast.13, f32[]{:T(128)} %bitcast), kind=kLoop, calls=%fused_computation.32 | loop fusion | flops 10485760 | bytes 12582920 | tf_op jit(solution)/shard_map/stack | solution.py:89
  151.7 2.4 %pad_maximum_fusion = bf16[2,1,1,1024,1024]{4,3,2,1,0:T(8,128)(2,1)} fusion(bf16[1,1,1,1024,1024]{4,3,2,1,0:T(8,128)(2,1)S(1)} %get-tuple-element.257, bf16[1,1,1,1024,1024]{4,3,2,1,0:T(8,128)(2,1)S(1)} %get-tuple-element.256), kind=kLoop, calls=%fused_computation.27 | loop fusion | flops 2097152 | bytes 8388608 | tf_op jit(solution)/shard_map/stack | solution.py:89
  (69 shorter events, 14.1 us)
Async XLA Ops:
  6.5 23.2 %copy-start = (f32[2,2]{1,0:T(2,128)S(1)}, f32[2,2]{1,0:T(2,128)}, u32[]{:S(2)}) copy-start(f32[2,2]{1,0:T(2,128)} %param.9) | copy-start | bytes 52
  6.5 34.0 %all-gather.8.cloned.1.call-start = ((), (), s32[]{:S(2)}) async-start(), calls=%async_computation | async-start | bytes 2621440 | tf_op jit(solution)/shard_map/all_gather | solution.py:14
  9.5 33.2 %copy-start.3 = (s32[32]{0:T(128)S(1)}, s32[32]{0:T(128)}, u32[]{:S(2)}) copy-start(s32[32]{0:T(128)} %param.8) | copy-start | bytes 388
  10.8 15.0 %collective-permute-start.2 = (bf16[2,1,128,1024]{3,2,1,0:T(8,128)(2,1)S(1)}, bf16[2,1,128,1024]{3,2,1,0:T(8,128)(2,1)S(1)}, u32[]{:S(2)}, u32[]{:S(2)}) collective-permute-start(bf16[2,1,128,1024]{3,2,1,0:T(8,128)(2,1)S(1)} %select_bitcast_fusion), channel_id=1, source_target_pairs={{0,1},{1,0},{2,3},{3,2},{4,5},{5,4},{6,7},{7,6},{8,9},{9,8},{10,11... | collective-permute-start | bytes 1572872 | tf_op jit(solution)/shard_map/ppermute | solution.py:24
  27.1 13.3 %collective-permute-start.3 = (bf16[2,1,128,1024]{3,2,1,0:T(8,128)(2,1)S(1)}, bf16[2,1,128,1024]{3,2,1,0:T(8,128)(2,1)S(1)}, u32[]{:S(2)}, u32[]{:S(2)}) collective-permute-start(bf16[2,1,128,1024]{3,2,1,0:T(8,128)(2,1)S(1)} %fusion.40), channel_id=1, source_target_pairs={{0,2},{2,0},{1,3},{3,1},{4,6},{6,4},{5,7},{7,5},{8,10},{10,8},{9,1... | collective-permute-start | bytes 1572872 | tf_op jit(solution)/shard_map/ppermute | solution.py:24
  42.7 30.3 %all-gather.10.cloned.1.call-start = ((), (), s32[]{:S(2)}) async-start(), calls=%async_computation.1 | async-start | bytes 2621440 | tf_op jit(solution)/shard_map/while/body/eval_jaxpr/all_gather | solution.py:14
  47.6 12.4 %collective-permute-start = (bf16[2,1,128,1024]{3,2,1,0:T(8,128)(2,1)S(1)}, bf16[2,1,128,1024]{3,2,1,0:T(8,128)(2,1)S(1)}, u32[]{:S(2)}, u32[]{:S(2)}) collective-permute-start(bf16[2,1,128,1024]{3,2,1,0:T(8,128)(2,1)S(1)} %dynamic-slice_select_fusion.6), channel_id=1, source_target_pairs={{0,1},{1,0},{2,3},{3,2},{4,5},{5,4},{6,7},{7,6},{8,9},{9,8},{10,11... | collective-permute-start | bytes 1572872 | tf_op jit(solution)/shard_map/while/body/eval_jaxpr/ppermute | solution.py:24
  51.3 11.3 %slice-start = ((s8[8388608]{0:T(1024)(128)(4,1)}), s8[4194304]{0:T(1024)(128)(4,1)S(1)}, s32[]{:S(2)}) async-start(s8[8388608]{0:T(1024)(128)(4,1)} %bitcast.97), calls=%async_computation.2 | async-start | bytes 8388608 | tf_op jit(solution)/shard_map/while
  52.0 10.6 %slice-start.1 = ((s8[8388608]{0:T(1024)(128)(4,1)}), s8[4194304]{0:T(1024)(128)(4,1)S(1)}, s32[]{:S(2)}) async-start(s8[8388608]{0:T(1024)(128)(4,1)} %bitcast.97), calls=%async_computation.3 | async-start | bytes 8388608 | tf_op jit(solution)/shard_map/while
  61.3 11.5 %collective-permute-start.1 = (bf16[2,1,128,1024]{3,2,1,0:T(8,128)(2,1)S(1)}, bf16[2,1,128,1024]{3,2,1,0:T(8,128)(2,1)S(1)}, u32[]{:S(2)}, u32[]{:S(2)}) collective-permute-start(bf16[2,1,128,1024]{3,2,1,0:T(8,128)(2,1)S(1)} %fusion.62), channel_id=1, source_target_pairs={{0,2},{2,0},{1,3},{3,1},{4,6},{6,4},{5,7},{7,5},{8,10},{10,8},{9,1... | collective-permute-start | bytes 1572872 | tf_op jit(solution)/shard_map/while/body/eval_jaxpr/ppermute | solution.py:24
  65.2 3.2 %copy-start.2 = (f32[2,1,1024,1024]{3,2,1,0:T(8,128)}, f32[2,1,1024,1024]{3,2,1,0:T(8,128)S(1)}, u32[]{:S(2)}) copy-start(f32[2,1,1024,1024]{3,2,1,0:T(8,128)S(1)} %maximum_add_fusion.3) | copy-start | bytes 25165828 | tf_op jit(solution)/shard_map/while
  75.0 28.5 %all-gather.10.cloned.1.call-start = ((), (), s32[]{:S(2)}) async-start(), calls=%async_computation.1 | async-start | bytes 2621440 | tf_op jit(solution)/shard_map/while/body/eval_jaxpr/all_gather | solution.py:14
  79.9 11.3 %collective-permute-start = (bf16[2,1,128,1024]{3,2,1,0:T(8,128)(2,1)S(1)}, bf16[2,1,128,1024]{3,2,1,0:T(8,128)(2,1)S(1)}, u32[]{:S(2)}, u32[]{:S(2)}) collective-permute-start(bf16[2,1,128,1024]{3,2,1,0:T(8,128)(2,1)S(1)} %dynamic-slice_select_fusion.6), channel_id=1, source_target_pairs={{0,1},{1,0},{2,3},{3,2},{4,5},{5,4},{6,7},{7,6},{8,9},{9,8},{10,11... | collective-permute-start | bytes 1572872 | tf_op jit(solution)/shard_map/while/body/eval_jaxpr/ppermute | solution.py:24
  83.1 11.0 %slice-start = ((s8[8388608]{0:T(1024)(128)(4,1)}), s8[4194304]{0:T(1024)(128)(4,1)S(1)}, s32[]{:S(2)}) async-start(s8[8388608]{0:T(1024)(128)(4,1)} %bitcast.97), calls=%async_computation.2 | async-start | bytes 8388608 | tf_op jit(solution)/shard_map/while
  83.8 10.3 %slice-start.1 = ((s8[8388608]{0:T(1024)(128)(4,1)}), s8[4194304]{0:T(1024)(128)(4,1)S(1)}, s32[]{:S(2)}) async-start(s8[8388608]{0:T(1024)(128)(4,1)} %bitcast.97), calls=%async_computation.3 | async-start | bytes 8388608 | tf_op jit(solution)/shard_map/while
  92.5 10.7 %collective-permute-start.1 = (bf16[2,1,128,1024]{3,2,1,0:T(8,128)(2,1)S(1)}, bf16[2,1,128,1024]{3,2,1,0:T(8,128)(2,1)S(1)}, u32[]{:S(2)}, u32[]{:S(2)}) collective-permute-start(bf16[2,1,128,1024]{3,2,1,0:T(8,128)(2,1)S(1)} %fusion.62), channel_id=1, source_target_pairs={{0,2},{2,0},{1,3},{3,1},{4,6},{6,4},{5,7},{7,5},{8,10},{10,8},{9,1... | collective-permute-start | bytes 1572872 | tf_op jit(solution)/shard_map/while/body/eval_jaxpr/ppermute | solution.py:24
  96.6 3.2 %copy-start.2 = (f32[2,1,1024,1024]{3,2,1,0:T(8,128)}, f32[2,1,1024,1024]{3,2,1,0:T(8,128)S(1)}, u32[]{:S(2)}) copy-start(f32[2,1,1024,1024]{3,2,1,0:T(8,128)S(1)} %maximum_add_fusion.3) | copy-start | bytes 25165828 | tf_op jit(solution)/shard_map/while
  105.4 31.2 %all-gather.10.cloned.1.call-start = ((), (), s32[]{:S(2)}) async-start(), calls=%async_computation.1 | async-start | bytes 2621440 | tf_op jit(solution)/shard_map/while/body/eval_jaxpr/all_gather | solution.py:14
  110.3 12.8 %collective-permute-start = (bf16[2,1,128,1024]{3,2,1,0:T(8,128)(2,1)S(1)}, bf16[2,1,128,1024]{3,2,1,0:T(8,128)(2,1)S(1)}, u32[]{:S(2)}, u32[]{:S(2)}) collective-permute-start(bf16[2,1,128,1024]{3,2,1,0:T(8,128)(2,1)S(1)} %dynamic-slice_select_fusion.6), channel_id=1, source_target_pairs={{0,1},{1,0},{2,3},{3,2},{4,5},{5,4},{6,7},{7,6},{8,9},{9,8},{10,11... | collective-permute-start | bytes 1572872 | tf_op jit(solution)/shard_map/while/body/eval_jaxpr/ppermute | solution.py:24
  114.3 11.7 %slice-start = ((s8[8388608]{0:T(1024)(128)(4,1)}), s8[4194304]{0:T(1024)(128)(4,1)S(1)}, s32[]{:S(2)}) async-start(s8[8388608]{0:T(1024)(128)(4,1)} %bitcast.97), calls=%async_computation.2 | async-start | bytes 8388608 | tf_op jit(solution)/shard_map/while
  115.0 11.0 %slice-start.1 = ((s8[8388608]{0:T(1024)(128)(4,1)}), s8[4194304]{0:T(1024)(128)(4,1)S(1)}, s32[]{:S(2)}) async-start(s8[8388608]{0:T(1024)(128)(4,1)} %bitcast.97), calls=%async_computation.3 | async-start | bytes 8388608 | tf_op jit(solution)/shard_map/while
  124.4 12.0 %collective-permute-start.1 = (bf16[2,1,128,1024]{3,2,1,0:T(8,128)(2,1)S(1)}, bf16[2,1,128,1024]{3,2,1,0:T(8,128)(2,1)S(1)}, u32[]{:S(2)}, u32[]{:S(2)}) collective-permute-start(bf16[2,1,128,1024]{3,2,1,0:T(8,128)(2,1)S(1)} %fusion.62), channel_id=1, source_target_pairs={{0,2},{2,0},{1,3},{3,1},{4,6},{6,4},{5,7},{7,5},{8,10},{10,8},{9,1... | collective-permute-start | bytes 1572872 | tf_op jit(solution)/shard_map/while/body/eval_jaxpr/ppermute | solution.py:24
  128.5 3.2 %copy-start.2 = (f32[2,1,1024,1024]{3,2,1,0:T(8,128)}, f32[2,1,1024,1024]{3,2,1,0:T(8,128)S(1)}, u32[]{:S(2)}) copy-start(f32[2,1,1024,1024]{3,2,1,0:T(8,128)S(1)} %maximum_add_fusion.3) | copy-start | bytes 25165828 | tf_op jit(solution)/shard_map/while
  140.0 3.6 %slice-start.2 = ((s8[8388608]{0:T(1024)(128)(4,1)}), s8[4194304]{0:T(1024)(128)(4,1)S(1)}, s32[]{:S(2)}) async-start(s8[8388608]{0:T(1024)(128)(4,1)} %bitcast.99), calls=%async_computation.4 | async-start | bytes 8388608
  140.7 4.4 %slice-start.3 = ((s8[8388608]{0:T(1024)(128)(4,1)}), s8[4194304]{0:T(1024)(128)(4,1)S(1)}, s32[]{:S(2)}) async-start(s8[8388608]{0:T(1024)(128)(4,1)} %bitcast.99), calls=%async_computation.5 | async-start | bytes 8388608
  151.7 2.4 %copy-start.1 = (f32[2,2]{1,0:T(2,128)S(1)}, f32[2,2]{1,0:T(2,128)}, u32[]{:S(2)}) copy-start(f32[2,2]{1,0:T(2,128)} %param.9) | copy-start | bytes 52
Sparse Core Ops, SparseCore 0:
  9.7 25.2 all-gather.7
  46.5 23.7 all-gather.9
  78.8 23.3 all-gather.9
  109.2 22.6 all-gather.9
